TPU v7x, 32 devices: a whole 2x2x4 slice. The times are simulated.
32 devices in a mesh: dom: 8 (over y, x, core), sub: 4 (over z).
Axes of the slice: x: 2, y: 2, z: 4, core: 2. Of those that a mesh axis runs over, the one named last changes fastest.
Arguments:
- start_dofs: float32 [140, 8192], P(None, ('dom', 'sub')), may hold values from -6 to 6
- inv_jac: float32 [9, 8192], P(None, ('dom', 'sub')), may hold values from -2 to 2
- normals: float32 [12, 8192], P(None, ('dom', 'sub')), may hold values from -3.5 to 3.5
- bulk_modulus: float32 [8192], P(('dom', 'sub')), may hold values from 0.5 to 2
- density: float32 [8192], P(('dom', 'sub')), may hold values from 0.5 to 2
- deriv_mats: float32 [3, 35, 35], replicated, may hold values from -1 to 1
- face_proj: float32 [4, 15, 35], replicated, may hold values from -1 to 1
- face_lift: float32 [4, 35, 15], replicated, may hold values from -1 to 1
- cluster: int32 [8192], P(('dom', 'sub')), may hold values from 0 to 1, as said below
- pml_flags: int32 [8192], P(('dom', 'sub')), may hold values 0 or 1
- neighbours: int32 [4, 8192], P(None, ('dom', 'sub')), may hold values from 0 to 1343, as said below
- dom_send: int32 [64, 96], P(('dom', 'sub')), may hold values from 0 to 1023, as said below
- sub_send: int32 [128, 32], P(('dom', 'sub')), may hold values from 0 to 1022, as said below
Outputs:
- final_dofs: float32 [140, 8192], P(None, ('dom', 'sub'))
Inputs may be any that keep to these rules, and one draw needn't show every extreme that they name: `cluster`: on every device the fine elements come first among its 256 elements; a device holds at most 64 of them, and some device exactly 64. `neighbours`: each face names one column of its device's trace pool. Own faces that are not listed for sending name each other in pairs. The face at place j of dom_send row 0 names place j of the block from the device before, the one at place j of row 1 place j of the block from the device after; the face at place j of the sub_send row for device b names place j of the block from b, or place j + 1 - 2 (j % 2) when b is the device itself. `dom_send`: together with its sub_send rows, the rows of one device list distinct columns of its own faces; every device lists its last face column here. `sub_send`: together with its dom_send rows, the rows of one device list distinct columns of its own faces; every device lists its second-to-last face column here.
All inputs are finite; a program needn't handle non-finite values. No bound on the sum of `pml_flags` on one device may be relied on, other than what follows from the above.
Results may differ from a plain program's by a relative error of at most 0.0003.
Values sent between devices are 32-bit elements; how exact they have to be, the bound alone decides.
No kernel may reach another device: no remote copies, remote signals or barrier semaphores. Data moves between devices by JAX's collectives and lax.ppermute only.
A program may use at most 64 MiB of HBM per device.

v0:
```python
import math
import jax
import jax.numpy as jnp
from jax import lax
from jax.sharding import PartitionSpec as P

NQ = 4
NB = 35
ORDER = 5
SUBSTEPS = 4
exact_dots = lax.Precision.HIGHEST
step_size = 0.8
sigma_pml = 1.5


def from_behind(shard, axis, by):
    peers = lax.axis_size(axis)
    pairs = [(i, i + by) for i in range(peers) if 0 <= i + by < peers]
    return lax.ppermute(shard, axis, pairs)


def apply_operator(coeffs, material):
    inv_jac, bulk_modulus, density, damping, deriv_mats = material
    n_basis = deriv_mats.shape[1]
    pressure = coeffs[0]
    velocity = coeffs[1:]
    stacked = deriv_mats.reshape(3 * n_basis, n_basis)
    d_press = jnp.dot(stacked, pressure, precision=exact_dots).reshape(3, n_basis, -1)
    jacobian = inv_jac.reshape(3, 3, -1)
    gradient = jnp.sum(jacobian[:, :, None, :] * d_press[:, None, :, :], axis=0)
    mixed_vel = jnp.sum(jacobian[:, :, None, :] * velocity[None, :, :, :], axis=1)
    joined = jnp.transpose(deriv_mats, (1, 0, 2)).reshape(n_basis, 3 * n_basis)
    diverg = jnp.dot(joined, mixed_vel.reshape(3 * n_basis, -1), precision=exact_dots)
    press_rate = -bulk_modulus * diverg - damping * pressure
    veloc_rate = -gradient / density - damping * velocity
    return jnp.concatenate([press_rate[None], veloc_rate], axis=0)


def taylor(coeffs, material):
    deriv_terms = [coeffs]
    for power in range(ORDER - 1):
        deriv_terms.append(apply_operator(deriv_terms[-1], material))
    return deriv_terms


def integrate(deriv_terms, start_time, end_time):
    summed = None
    for power, taylor_term in enumerate(deriv_terms):
        weight = (end_time ** (power + 1) - start_time ** (power + 1)) / math.factorial(power + 1)
        scaled = weight * taylor_term
        summed = scaled if summed is None else summed + scaled
    return summed


def face_traces(coeffs, face_proj):
    face_parts = []
    for face_idx in range(4):
        traced = jnp.einsum("kb,qbe->kqe", face_proj[face_idx], coeffs, precision=exact_dots)
        face_parts.append(traced.reshape(-1, coeffs.shape[2]))
    return jnp.concatenate(face_parts, axis=1)


def corrections(own_traces, nbr_traces, normals, bulk_modulus, density, face_lift):
    n_elem = normals.shape[1]
    n_face = face_lift.shape[2]
    jump_all = (nbr_traces - own_traces).reshape(n_face, 4, 4, n_elem)
    jump_press = jump_all[:, 0]
    jump_vel = jump_all[:, 1:]
    facing = jnp.transpose(normals.reshape(4, 3, n_elem), (1, 0, 2))
    normal_flow = jnp.sum(facing[None] * jump_vel, axis=1)
    sound_speed = jnp.sqrt(bulk_modulus / density)
    penalty = sound_speed * jnp.sqrt(jnp.sum(facing * facing, axis=0))
    flux_press = 0.5 * (bulk_modulus * normal_flow - penalty * jump_press)
    flux_veloc = 0.5 * (facing[None] * jump_press[:, None] / density - penalty * jump_vel)
    flux_all = jnp.concatenate([flux_press[:, None], flux_veloc], axis=1)
    return jnp.einsum("fbk,kqfe->qbe", face_lift, flux_all, precision=exact_dots)


def gather_faces(own_traces, dom_send, sub_send):
    n_chan = own_traces.shape[0]
    n_sub = sub_send.shape[0]
    sub_width = sub_send.shape[1]
    dom_out = jnp.stack(
        [jnp.take(own_traces, dom_send[0], axis=1), jnp.take(own_traces, dom_send[1], axis=1)]
    )
    sub_out = jnp.take(own_traces, sub_send.reshape(-1), axis=1).reshape(n_chan, n_sub, sub_width)
    sub_in = lax.all_to_all(sub_out, "sub", split_axis=1, concat_axis=1, tiled=True).reshape(
        n_chan, n_sub * sub_width
    )
    from_below = from_behind(dom_out[1], "dom", 1)
    from_above = from_behind(dom_out[0], "dom", -1)
    return jnp.concatenate([own_traces, from_below, from_above, sub_in], axis=1)


def body(
    start_dofs,
    inv_jac,
    normals,
    bulk_modulus,
    density,
    deriv_mats,
    face_proj,
    face_lift,
    cluster,
    pml_flags,
    neighbours,
    dom_send,
    sub_send,
):
    n_elem = start_dofs.shape[1]
    dofs_zero = start_dofs.reshape(NQ, NB, n_elem)
    damping = sigma_pml * pml_flags.astype(jnp.float32)
    fine_mask = cluster == 1
    material = (inv_jac, bulk_modulus, density, damping, deriv_mats)
    coarse_terms = taylor(dofs_zero, material)
    sub_dt = step_size / SUBSTEPS
    head_material = (inv_jac, bulk_modulus, density, damping, deriv_mats)
    work_state = jnp.where(fine_mask, dofs_zero, 0.0)
    for sub_step in range(SUBSTEPS):
        coarse_part = integrate(coarse_terms, sub_step * sub_dt, (sub_step + 1) * sub_dt)
        work_head = work_state
        fine_part = integrate(taylor(work_head, head_material), 0.0, sub_dt)
        published = jnp.where(fine_mask, fine_part, coarse_part)
        own_traces = face_traces(published, face_proj)
        trace_pool = gather_faces(own_traces, dom_send, sub_send)
        nbr_traces = jnp.take(trace_pool, neighbours.reshape(-1), axis=1)
        lifted = corrections(own_traces, nbr_traces, normals, bulk_modulus, density, face_lift)
        coarse_next = work_state + lifted
        stepped = work_head + apply_operator(fine_part, head_material) - lifted
        head_next = jnp.where(fine_mask, stepped, coarse_next)
        work_state = head_next
    full_step = integrate(coarse_terms, 0.0, step_size)
    coarse_out = dofs_zero + apply_operator(full_step, material) - work_state
    return jnp.where(fine_mask, work_state, coarse_out).reshape(NQ * NB, n_elem)


def solution(mesh):
    in_specs = (
        P(None, ("dom", "sub")),
        P(None, ("dom", "sub")),
        P(None, ("dom", "sub")),
        P(("dom", "sub")),
        P(("dom", "sub")),
        P(),
        P(),
        P(),
        P(("dom", "sub")),
        P(("dom", "sub")),
        P(None, ("dom", "sub")),
        P(("dom", "sub"), None),
        P(("dom", "sub"), None),
    )
    out_specs = P(None, ("dom", "sub"))
    return jax.shard_map(body, mesh=mesh, in_specs=in_specs, out_specs=out_specs, check_vma=False)
```

profile of v0, /device:TPU:11, one launch (start us, length us, event | category | flops | bytes accessed | tf_op | source)
XLA Modules:
  0.0 125.4 jit_solution(3070285738189939827)
XLA Ops:
  0.0 0.8 reshape.421
  0.8 0.9 reshape.662
  1.7 0.9 slice.126
  7.1 0.8 slice-done
  10.8 0.8 multiply_reduce_fusion.1
  16.8 4.9 %all-to-all-start = ((f32[4,1,1920]{2,1,0:T(1,128)}), f32[4,1,1920]{2,1,0:T(1,128)S(1)}, u32[]{:S(2)}, u32[]{:S(2)}) async-start(f32[4,1,1920]{2,1,0:T(1,128)} %reshape.663), calls=%async_computation | async-start | bytes 61440 | tf_op jit(solution)/shard_map/all_to_all | solution.py:87
  23.1 4.2 %collective-permute-start = (f32[60,96]{0,1:T(8,128)S(1)}, f32[60,96]{0,1:T(8,128)S(1)}, u32[]{:S(2)}, u32[]{:S(2)}) collective-permute-start(f32[60,96]{0,1:T(8,128)S(1)} %select_bitcast_fusion.7), channel_id=1, source_target_pairs={{0,4},{4,8},{8,12},{12,16},{16,20},{20,24},{24,28},{1,5},{5,9},{9,... | collective-permute-start | bytes 69128 | tf_op jit(solution)/shard_map/ppermute | solution.py:19
  28.7 1.9 %collective-permute-start.1 = (f32[60,96]{0,1:T(8,128)}, f32[60,96]{0,1:T(8,128)}, u32[]{:S(2)}, u32[]{:S(2)}) collective-permute-start(f32[60,96]{0,1:T(8,128)} %select_bitcast_fusion.6), channel_id=1, source_target_pairs={{4,0},{8,4},{12,8},{16,12},{20,16},{24,20},{28,24},{5,1},{9,5},{13... | collective-permute-start | bytes 69128 | tf_op jit(solution)/shard_map/ppermute | solution.py:19
  33.2 2.1 %collective-permute-done.1 = f32[60,96]{0,1:T(8,128)} collective-permute-done((f32[60,96]{0,1:T(8,128)}, f32[60,96]{0,1:T(8,128)}, u32[]{:S(2)}, u32[]{:S(2)}) %collective-permute-start.1) | collective-permute-done | bytes 23072 | tf_op jit(solution)/shard_map/ppermute | solution.py:19
  35.3 0.8 constant_dynamic-update-slice_fusion.1
  37.4 2.8 %gather_fusion.3 = f32[1024,60]{1,0:T(8,128)S(1)} fusion(f32[60,1344]{0,1:T(8,128)S(1)} %constant_dynamic-update-slice_fusion, s32[1024]{0:T(1024)S(1)} %get-tuple-element.102), kind=kCustom, calls=%fused_computation.2.clone | custom fusion | bytes 495616 | tf_op jit(solution)/shard_map/jit(_take)/gather | solution.py:126
  46.6 0.7 gather_fusion.5
  48.1 0.8 gather_fusion.6
  50.9 4.5 %all-to-all-start.1 = ((f32[4,1,1920]{2,1,0:T(1,128)}), f32[4,1,1920]{2,1,0:T(1,128)S(1)}, u32[]{:S(2)}, u32[]{:S(2)}) async-start(f32[4,1,1920]{2,1,0:T(1,128)} %reshape.665), calls=%async_computation.1 | async-start | bytes 61440 | tf_op jit(solution)/shard_map/all_to_all | solution.py:87
  55.4 3.0 %collective-permute-start.2 = (f32[60,96]{0,1:T(8,128)S(1)}, f32[60,96]{0,1:T(8,128)S(1)}, u32[]{:S(2)}, u32[]{:S(2)}) collective-permute-start(f32[60,96]{0,1:T(8,128)S(1)} %select_bitcast_fusion.5), channel_id=1, source_target_pairs={{0,4},{4,8},{8,12},{12,16},{16,20},{20,24},{24,28},{1,5},{5,9},{9,... | collective-permute-start | bytes 69128 | tf_op jit(solution)/shard_map/ppermute | solution.py:19
  58.4 1.9 %collective-permute-start.3 = (f32[60,96]{0,1:T(8,128)S(1)}, f32[60,96]{0,1:T(8,128)S(1)}, u32[]{:S(2)}, u32[]{:S(2)}) collective-permute-start(f32[60,96]{0,1:T(8,128)S(1)} %select_bitcast_fusion.4), channel_id=1, source_target_pairs={{4,0},{8,4},{12,8},{16,12},{20,16},{24,20},{28,24},{5,1},{9,5},{13... | collective-permute-start | bytes 69128 | tf_op jit(solution)/shard_map/ppermute | solution.py:19
  60.4 4.3 %collective-permute-done.3 = f32[60,96]{0,1:T(8,128)S(1)} collective-permute-done((f32[60,96]{0,1:T(8,128)S(1)}, f32[60,96]{0,1:T(8,128)S(1)}, u32[]{:S(2)}, u32[]{:S(2)}) %collective-permute-start.3) | collective-permute-done | bytes 23072 | tf_op jit(solution)/shard_map/ppermute | solution.py:19
  65.5 2.8 %gather_fusion.7 = f32[1024,60]{1,0:T(8,128)S(1)} fusion(f32[60,1344]{0,1:T(8,128)S(1)} %constant_dynamic-update-slice_fusion.7, s32[1024]{0:T(1024)S(1)} %get-tuple-element.102), kind=kCustom, calls=%fused_computation.13.clone | custom fusion | bytes 495616 | tf_op jit(solution)/shard_map/jit(_take)/gather | solution.py:126
  74.1 0.7 gather_fusion.9
  75.6 0.8 gather_fusion.10
  78.3 4.5 %all-to-all-start.2 = ((f32[4,1,1920]{2,1,0:T(1,128)}), f32[4,1,1920]{2,1,0:T(1,128)S(1)}, u32[]{:S(2)}, u32[]{:S(2)}) async-start(f32[4,1,1920]{2,1,0:T(1,128)} %reshape.667), calls=%async_computation.2 | async-start | bytes 61440 | tf_op jit(solution)/shard_map/all_to_all | solution.py:87
  82.8 2.4 %collective-permute-start.4 = (f32[60,96]{0,1:T(8,128)S(1)}, f32[60,96]{0,1:T(8,128)S(1)}, u32[]{:S(2)}, u32[]{:S(2)}) collective-permute-start(f32[60,96]{0,1:T(8,128)S(1)} %select_bitcast_fusion.3), channel_id=1, source_target_pairs={{0,4},{4,8},{8,12},{12,16},{16,20},{20,24},{24,28},{1,5},{5,9},{9,... | collective-permute-start | bytes 69128 | tf_op jit(solution)/shard_map/ppermute | solution.py:19
  85.3 1.9 %collective-permute-start.5 = (f32[60,96]{0,1:T(8,128)S(1)}, f32[60,96]{0,1:T(8,128)S(1)}, u32[]{:S(2)}, u32[]{:S(2)}) collective-permute-start(f32[60,96]{0,1:T(8,128)S(1)} %select_bitcast_fusion.2), channel_id=1, source_target_pairs={{4,0},{8,4},{12,8},{16,12},{20,16},{24,20},{28,24},{5,1},{9,5},{13... | collective-permute-start | bytes 69128 | tf_op jit(solution)/shard_map/ppermute | solution.py:19
  87.3 4.3 %collective-permute-done.5 = f32[60,96]{0,1:T(8,128)S(1)} collective-permute-done((f32[60,96]{0,1:T(8,128)S(1)}, f32[60,96]{0,1:T(8,128)S(1)}, u32[]{:S(2)}, u32[]{:S(2)}) %collective-permute-start.5) | collective-permute-done | bytes 23072 | tf_op jit(solution)/shard_map/ppermute | solution.py:19
  92.4 2.8 %gather_fusion.11 = f32[1024,60]{1,0:T(8,128)S(1)} fusion(f32[60,1344]{0,1:T(8,128)S(1)} %constant_dynamic-update-slice_fusion.14, s32[1024]{0:T(1024)S(1)} %get-tuple-element.102), kind=kCustom, calls=%fused_computation.14.clone | custom fusion | bytes 495616 | tf_op jit(solution)/shard_map/jit(_take)/gather | solution.py:126
  103.0 0.7 gather_fusion.13
  104.5 0.8 gather_fusion.14
  106.7 4.5 %all-to-all-start.3 = ((f32[4,1,1920]{2,1,0:T(1,128)}), f32[4,1,1920]{2,1,0:T(1,128)S(1)}, u32[]{:S(2)}, u32[]{:S(2)}) async-start(f32[4,1,1920]{2,1,0:T(1,128)} %reshape.669), calls=%async_computation.3 | async-start | bytes 61440 | tf_op jit(solution)/shard_map/all_to_all | solution.py:87
  111.2 2.4 %collective-permute-start.6 = (f32[60,96]{0,1:T(8,128)S(1)}, f32[60,96]{0,1:T(8,128)S(1)}, u32[]{:S(2)}, u32[]{:S(2)}) collective-permute-start(f32[60,96]{0,1:T(8,128)S(1)} %select_bitcast_fusion.1), channel_id=1, source_target_pairs={{0,4},{4,8},{8,12},{12,16},{16,20},{20,24},{24,28},{1,5},{5,9},{9,... | collective-permute-start | bytes 69128 | tf_op jit(solution)/shard_map/ppermute | solution.py:19
  113.7 1.9 %collective-permute-start.7 = (f32[60,96]{0,1:T(8,128)S(1)}, f32[60,96]{0,1:T(8,128)S(1)}, u32[]{:S(2)}, u32[]{:S(2)}) collective-permute-start(f32[60,96]{0,1:T(8,128)S(1)} %select_bitcast_fusion), channel_id=1, source_target_pairs={{4,0},{8,4},{12,8},{16,12},{20,16},{24,20},{28,24},{5,1},{9,5},{13... | collective-permute-start | bytes 69128 | tf_op jit(solution)/shard_map/ppermute | solution.py:19
  115.7 4.3 %collective-permute-done.7 = f32[60,96]{0,1:T(8,128)S(1)} collective-permute-done((f32[60,96]{0,1:T(8,128)S(1)}, f32[60,96]{0,1:T(8,128)S(1)}, u32[]{:S(2)}, u32[]{:S(2)}) %collective-permute-start.7) | collective-permute-done | bytes 23072 | tf_op jit(solution)/shard_map/ppermute | solution.py:19
  120.8 2.8 %gather_fusion.15 = f32[1024,60]{1,0:T(8,128)S(1)} fusion(f32[60,1344]{0,1:T(8,128)S(1)} %constant_dynamic-update-slice_fusion.21, s32[1024]{0:T(1024)S(1)} %get-tuple-element.102), kind=kCustom, calls=%fused_computation.15.clone | custom fusion | bytes 495616 | tf_op jit(solution)/shard_map/jit(_take)/gather | solution.py:126
  (400 shorter events, 49.0 us)
Async XLA Ops:
  0.8 15.2 %copy-start.27 = (pred[128]{0:T(512)(128)(4,1)}, pred[128]{0:T(512)(128)(4,1)S(1)}, u32[]{:S(2)}) copy-start(pred[128]{0:T(512)(128)(4,1)S(1)} %compare_and_fusion.1) | copy-start | bytes 388
  0.8 1.8 %copy-start.1 = (f32[140,256]{1,0:T(8,128)S(1)}, f32[140,256]{1,0:T(8,128)}, u32[]{:S(2)}) copy-start(f32[140,256]{1,0:T(8,128)} %param.19) | copy-start | bytes 430084
  1.7 0.9 copy-start
  2.9 0.7 copy-start.18
  7.0 0.9 slice-start
  9.3 0.8 copy-start.13
  9.3 0.9 copy-start.3
  10.0 5.2 %copy-start.25 = (s32[1024]{0:T(1024)}, s32[1024]{0:T(1024)S(1)}, u32[]{:S(2)}) copy-start(s32[1024]{0:T(1024)S(1)} %pad_clamp_fusion) | copy-start | bytes 12292
  10.1 62.1 %copy-start.11 = (f32[1,15,35]{2,0,1:T(1,128)}, f32[1,15,35]{2,0,1:T(1,128)S(1)}, u32[]{:S(2)}) copy-start(f32[1,15,35]{2,0,1:T(1,128)S(1)} %get-tuple-element.91) | copy-start | bytes 6304
  10.1 62.3 %copy-start.9 = (f32[1,15,35]{2,0,1:T(1,128)}, f32[1,15,35]{2,0,1:T(1,128)S(1)}, u32[]{:S(2)}) copy-start(f32[1,15,35]{2,0,1:T(1,128)S(1)} %get-tuple-element.92) | copy-start | bytes 6304
  10.1 62.5 %copy-start.7 = (f32[1,15,35]{2,0,1:T(1,128)}, f32[1,15,35]{2,0,1:T(1,128)S(1)}, u32[]{:S(2)}) copy-start(f32[1,15,35]{2,0,1:T(1,128)S(1)} %get-tuple-element.93) | copy-start | bytes 6304
  16.8 4.9 %copy-start.31 = (s32[2,96]{1,0:T(2,128)S(1)}, s32[2,96]{1,0:T(2,128)}, u32[]{:S(2)}) copy-start(s32[2,96]{1,0:T(2,128)} %param.30) | copy-start | bytes 2308
  16.8 19.3 %all-to-all-start = ((f32[4,1,1920]{2,1,0:T(1,128)}), f32[4,1,1920]{2,1,0:T(1,128)S(1)}, u32[]{:S(2)}, u32[]{:S(2)}) async-start(f32[4,1,1920]{2,1,0:T(1,128)} %reshape.663), calls=%async_computation | async-start | bytes 61440 | tf_op jit(solution)/shard_map/all_to_all | solution.py:87
  21.7 27.6 %copy-start.22 = (pred[96]{0:T(512)(128)(4,1)}, pred[96]{0:T(512)(128)(4,1)S(1)}, u32[]{:S(2)}) copy-start(pred[96]{0:T(512)(128)(4,1)S(1)} %get-tuple-element.59) | copy-start | bytes 292
  21.7 29.1 %copy-start.20 = (pred[96]{0:T(512)(128)(4,1)}, pred[96]{0:T(512)(128)(4,1)S(1)}, u32[]{:S(2)}) copy-start(pred[96]{0:T(512)(128)(4,1)S(1)} %get-tuple-element.98) | copy-start | bytes 292
  23.1 10.1 %collective-permute-start = (f32[60,96]{0,1:T(8,128)S(1)}, f32[60,96]{0,1:T(8,128)S(1)}, u32[]{:S(2)}, u32[]{:S(2)}) collective-permute-start(f32[60,96]{0,1:T(8,128)S(1)} %select_bitcast_fusion.7), channel_id=1, source_target_pairs={{0,4},{4,8},{8,12},{12,16},{16,20},{20,24},{24,28},{1,5},{5,9},{9,... | collective-permute-start | bytes 69128 | tf_op jit(solution)/shard_map/ppermute | solution.py:19
  28.7 6.6 %collective-permute-start.1 = (f32[60,96]{0,1:T(8,128)}, f32[60,96]{0,1:T(8,128)}, u32[]{:S(2)}, u32[]{:S(2)}) collective-permute-start(f32[60,96]{0,1:T(8,128)} %select_bitcast_fusion.6), channel_id=1, source_target_pairs={{4,0},{8,4},{12,8},{16,12},{20,16},{24,20},{28,24},{5,1},{9,5},{13... | collective-permute-start | bytes 69128 | tf_op jit(solution)/shard_map/ppermute | solution.py:19
  30.6 9.6 %copy-start.16 = (pred[1024]{0:T(1024)(128)(4,1)}, pred[1024]{0:T(1024)(128)(4,1)S(1)}, u32[]{:S(2)}) copy-start(pred[1024]{0:T(1024)(128)(4,1)S(1)} %compare_and_fusion) | copy-start | bytes 3076
  30.9 0.7 copy-start.19
  30.9 0.9 copy-start.6
  40.9 0.8 copy-start.5
  50.9 13.8 %all-to-all-start.1 = ((f32[4,1,1920]{2,1,0:T(1,128)}), f32[4,1,1920]{2,1,0:T(1,128)S(1)}, u32[]{:S(2)}, u32[]{:S(2)}) async-start(f32[4,1,1920]{2,1,0:T(1,128)} %reshape.665), calls=%async_computation.1 | async-start | bytes 61440 | tf_op jit(solution)/shard_map/all_to_all | solution.py:87
  55.4 5.0 %collective-permute-start.2 = (f32[60,96]{0,1:T(8,128)S(1)}, f32[60,96]{0,1:T(8,128)S(1)}, u32[]{:S(2)}, u32[]{:S(2)}) collective-permute-start(f32[60,96]{0,1:T(8,128)S(1)} %select_bitcast_fusion.5), channel_id=1, source_target_pairs={{0,4},{4,8},{8,12},{12,16},{16,20},{20,24},{24,28},{1,5},{5,9},{9,... | collective-permute-start | bytes 69128 | tf_op jit(solution)/shard_map/ppermute | solution.py:19
  58.4 6.3 %collective-permute-start.3 = (f32[60,96]{0,1:T(8,128)S(1)}, f32[60,96]{0,1:T(8,128)S(1)}, u32[]{:S(2)}, u32[]{:S(2)}) collective-permute-start(f32[60,96]{0,1:T(8,128)S(1)} %select_bitcast_fusion.4), channel_id=1, source_target_pairs={{4,0},{8,4},{12,8},{16,12},{20,16},{24,20},{28,24},{5,1},{9,5},{13... | collective-permute-start | bytes 69128 | tf_op jit(solution)/shard_map/ppermute | solution.py:19
  65.5 2.8 %copy-start.17 = (pred[1024]{0:T(1024)(128)(4,1)S(1)}, pred[1024]{0:T(1024)(128)(4,1)}, u32[]{:S(2)}) copy-start(pred[1024]{0:T(1024)(128)(4,1)} %copy-done.16) | copy-start | bytes 3076
  77.4 0.8 copy-start.21
  78.3 13.3 %all-to-all-start.2 = ((f32[4,1,1920]{2,1,0:T(1,128)}), f32[4,1,1920]{2,1,0:T(1,128)S(1)}, u32[]{:S(2)}, u32[]{:S(2)}) async-start(f32[4,1,1920]{2,1,0:T(1,128)} %reshape.667), calls=%async_computation.2 | async-start | bytes 61440 | tf_op jit(solution)/shard_map/all_to_all | solution.py:87
  82.8 4.4 %collective-permute-start.4 = (f32[60,96]{0,1:T(8,128)S(1)}, f32[60,96]{0,1:T(8,128)S(1)}, u32[]{:S(2)}, u32[]{:S(2)}) collective-permute-start(f32[60,96]{0,1:T(8,128)S(1)} %select_bitcast_fusion.3), channel_id=1, source_target_pairs={{0,4},{4,8},{8,12},{12,16},{16,20},{20,24},{24,28},{1,5},{5,9},{9,... | collective-permute-start | bytes 69128 | tf_op jit(solution)/shard_map/ppermute | solution.py:19
  85.3 6.3 %collective-permute-start.5 = (f32[60,96]{0,1:T(8,128)S(1)}, f32[60,96]{0,1:T(8,128)S(1)}, u32[]{:S(2)}, u32[]{:S(2)}) collective-permute-start(f32[60,96]{0,1:T(8,128)S(1)} %select_bitcast_fusion.2), channel_id=1, source_target_pairs={{4,0},{8,4},{12,8},{16,12},{20,16},{24,20},{28,24},{5,1},{9,5},{13... | collective-permute-start | bytes 69128 | tf_op jit(solution)/shard_map/ppermute | solution.py:19
  106.7 13.3 %all-to-all-start.3 = ((f32[4,1,1920]{2,1,0:T(1,128)}), f32[4,1,1920]{2,1,0:T(1,128)S(1)}, u32[]{:S(2)}, u32[]{:S(2)}) async-start(f32[4,1,1920]{2,1,0:T(1,128)} %reshape.669), calls=%async_computation.3 | async-start | bytes 61440 | tf_op jit(solution)/shard_map/all_to_all | solution.py:87
  111.2 4.4 %collective-permute-start.6 = (f32[60,96]{0,1:T(8,128)S(1)}, f32[60,96]{0,1:T(8,128)S(1)}, u32[]{:S(2)}, u32[]{:S(2)}) collective-permute-start(f32[60,96]{0,1:T(8,128)S(1)} %select_bitcast_fusion.1), channel_id=1, source_target_pairs={{0,4},{4,8},{8,12},{12,16},{16,20},{20,24},{24,28},{1,5},{5,9},{9,... | collective-permute-start | bytes 69128 | tf_op jit(solution)/shard_map/ppermute | solution.py:19
  113.7 6.3 %collective-permute-start.7 = (f32[60,96]{0,1:T(8,128)S(1)}, f32[60,96]{0,1:T(8,128)S(1)}, u32[]{:S(2)}, u32[]{:S(2)}) collective-permute-start(f32[60,96]{0,1:T(8,128)S(1)} %select_bitcast_fusion), channel_id=1, source_target_pairs={{4,0},{8,4},{12,8},{16,12},{20,16},{24,20},{28,24},{5,1},{9,5},{13... | collective-permute-start | bytes 69128 | tf_op jit(solution)/shard_map/ppermute | solution.py:19
  (15 other events, 10.0 us)
where the time goes:
time: 127 us; the launch traced here: 125 us
  local copies, waits for them, and re-layouts  42.8 us (34%)
  starting transfers between devices  38.3 us (30%)
  matrix products  17.1 us (13%)
  waiting for transfers between devices  15 us (12%)
  other arithmetic  9.86 us (8%)
  between operations  2.35 us (2%)
    ppermute x8, starting transfers between devices, from_behind(): return lax.ppermute(shard, axis, pairs)  19.8 us
    all_to_all x4, starting transfers between devices, gather_faces(): lax.all_to_all(sub_out, 'sub', split_axis=1, concat_axis=1, tiled=True)  18.5 us
    ppermute x8, waiting for transfers between devices, from_behind(): return lax.ppermute(shard, axis, pairs)  15 us
    unnamed x105, local copies, waits for them, and re-layouts  13.5 us
    gather x4, local copies, waits for them, and re-layouts, body(): nbr_traces = jnp.take(trace_pool, neighbours.reshape(-1), axis=1)  11.2 us
    dot_general x25, matrix products, apply_operator(): jnp.dot(joined, mixed_vel.reshape(3 * n_basis, -1), precision=exact_dots)  6.34 us
    dot_general x25, matrix products, apply_operator(): jnp.dot(stacked, pressure, precision=exact_dots).reshape(3, n_basis, -1)  5.98 us
    dot_general x16, matrix products, face_traces(): jnp.einsum('kb,qbe->kqe', face_proj[face_idx], coeffs, precision=exact_dots)  3.34 us
  transfers between devices with their start and end apart: 12, of which 4 were waited for; matrix products, arithmetic and copies ran while one was open for 3% of the time, Pallas kernels for 0%

commit v1 on v0

--- a/solution.py
+++ b/solution.py
@@ -11,6 +11,29 @@
 exact_dots = lax.Precision.HIGHEST
 step_size = 0.8
 sigma_pml = 1.5
+
+
+def cut_along(value, dim, size):
+    lengths = value.shape
+    blocks = value.reshape(*lengths[:dim], size, lengths[dim] // size, *lengths[dim + 1 :])
+    return jnp.moveaxis(blocks, dim, 0)
+
+
+def in_order(blocks, dim):
+    shape = list(blocks.shape[1:])
+    shape[dim] *= blocks.shape[0]
+    return jnp.moveaxis(blocks, 0, dim).reshape(shape)
+
+
+def swapped_with_each(x, axis, split_dim, concat_dim):
+    peers, place = (lax.axis_size(axis), lax.axis_index(axis))
+    tiles = cut_along(x, split_dim, peers)
+    outs = [tiles[place]]
+    for step in range(1, peers):
+        sent = tiles[place ^ step]
+        outs.append(lax.ppermute(sent, axis, [(i, i ^ step) for i in range(peers)]))
+    tiles = jnp.stack(outs)[place ^ jnp.arange(peers)]
+    return in_order(tiles, concat_dim)
 
 
 def from_behind(shard, axis, by):
@@ -84,9 +107,7 @@
         [jnp.take(own_traces, dom_send[0], axis=1), jnp.take(own_traces, dom_send[1], axis=1)]
     )
     sub_out = jnp.take(own_traces, sub_send.reshape(-1), axis=1).reshape(n_chan, n_sub, sub_width)
-    sub_in = lax.all_to_all(sub_out, "sub", split_axis=1, concat_axis=1, tiled=True).reshape(
-        n_chan, n_sub * sub_width
-    )
+    sub_in = swapped_with_each(sub_out, "sub", 1, 1).reshape(n_chan, n_sub * sub_width)
     from_below = from_behind(dom_out[1], "dom", 1)
     from_above = from_behind(dom_out[0], "dom", -1)
     return jnp.concatenate([own_traces, from_below, from_above, sub_in], axis=1)

time: 127 us -> 122 us (0.961)
  waiting for transfers between devices: 15 us -> 10.5 us
  local copies, waits for them, and re-layouts: 42.8 us -> 45.3 us
  other arithmetic: 9.86 us -> 8.09 us
    all_to_all x4 -> x0, starting transfers between devices: 18.5 us -> none  [gather_faces(): lax.all_to_all(sub_out, 'sub', split_axis=1, concat_axis=1, tiled=True)]
    ppermute x0 -> x12, starting transfers between devices: none -> 15.2 us  [swapped_with_each(): outs.append(lax.ppermute(sent, axis, [(i, i ^ step) for i in range(peers)]))]
    ppermute x8, waiting for transfers between devices: 15 us -> 10.5 us  [from_behind(): return lax.ppermute(shard, axis, pairs)]
    gather x0 -> x4, local copies, waits for them, and re-layouts: none -> 2.58 us  [swapped_with_each(): tiles = jnp.stack(outs)[place ^ jnp.arange(peers)]]
    all_to_all x4 -> x0, other arithmetic: 2.57 us -> none  [gather_faces(): lax.all_to_all(sub_out, 'sub', split_axis=1, concat_axis=1, tiled=True)]
    ppermute x8, starting transfers between devices: 19.8 us -> 22.3 us  [from_behind(): return lax.ppermute(shard, axis, pairs)]
    unnamed x105 -> x111, local copies, waits for them, and re-layouts: 13.5 us -> 14.4 us
  transfers between devices with their start and end apart: 12 -> 20, of which waited for: 4 -> 3; matrix products, arithmetic and copies ran while one was open for 3% -> 6% of each run, Pallas kernels for 0% -> 0%
where the time goes in v1:
time: 122 us; the launch traced here: 121 us
  local copies, waits for them, and re-layouts  45.3 us (37%)
  starting transfers between devices  37.5 us (31%)
  matrix products  17.1 us (14%)
  waiting for transfers between devices  10.5 us (9%)
  other arithmetic  8.09 us (7%)
  between operations  2.54 us (2%)
    ppermute x8, starting transfers between devices, from_behind(): return lax.ppermute(shard, axis, pairs)  22.3 us
    ppermute x12, starting transfers between devices, swapped_with_each(): outs.append(lax.ppermute(sent, axis, [(i, i ^ step) for i in range(peers)]))  15.2 us
    unnamed x111, local copies, waits for them, and re-layouts  14.4 us
    gather x4, local copies, waits for them, and re-layouts, body(): nbr_traces = jnp.take(trace_pool, neighbours.reshape(-1), axis=1)  11.2 us
    ppermute x8, waiting for transfers between devices, from_behind(): return lax.ppermute(shard, axis, pairs)  10.5 us
    dot_general x25, matrix products, apply_operator(): jnp.dot(joined, mixed_vel.reshape(3 * n_basis, -1), precision=exact_dots)  6.34 us
    dot_general x25, matrix products, apply_operator(): jnp.dot(stacked, pressure, precision=exact_dots).reshape(3, n_basis, -1)  5.99 us
    dot_general x16, matrix products, face_traces(): jnp.einsum('kb,qbe->kqe', face_proj[face_idx], coeffs, precision=exact_dots)  3.34 us
  transfers between devices with their start and end apart: 20, of which 3 were waited for; matrix products, arithmetic and copies ran while one was open for 6% of the time, Pallas kernels for 0%

profile of v1, /device:TPU:11, one launch (start us, length us, event | category | flops | bytes accessed | tf_op | source)
XLA Modules:
  0.0 120.9 jit_solution(12104310928022313319)
XLA Ops:
  0.8 0.8 reshape.714
  1.7 0.8 copy-done
  7.0 0.8 slice-done
  16.6 1.3 %collective-permute-start.4 = (f32[60,1,32]{0,2,1:T(8,128)}, f32[60,1,32]{0,2,1:T(8,128)S(1)}, u32[]{:S(2)}, u32[]{:S(2)}) collective-permute-start(f32[60,1,32]{0,2,1:T(8,128)} %get-tuple-element.104), channel_id=1, source_target_pairs={{0,3},{1,2},{2,1},{3,0},{4,7},{5,6},{6,5},{7,4},{8,11},{9,10},{10,... | collective-permute-start | bytes 23048 | tf_op jit(solution)/shard_map/ppermute | solution.py:34
  17.9 1.0 collective-permute-start.3
  18.9 1.2 collective-permute-start.2
  20.9 4.2 %collective-permute-start = (f32[60,96]{0,1:T(8,128)S(1)}, f32[60,96]{0,1:T(8,128)}, u32[]{:S(2)}, u32[]{:S(2)}) collective-permute-start(f32[60,96]{0,1:T(8,128)S(1)} %select_bitcast_fusion.7), channel_id=1, source_target_pairs={{0,4},{4,8},{8,12},{12,16},{16,20},{20,24},{24,28},{1,5},{5,9},{9,... | collective-permute-start | bytes 69128 | tf_op jit(solution)/shard_map/ppermute | solution.py:42
  26.4 2.1 %collective-permute-start.1 = (f32[60,96]{0,1:T(8,128)}, f32[60,96]{0,1:T(8,128)}, u32[]{:S(2)}, u32[]{:S(2)}) collective-permute-start(f32[60,96]{0,1:T(8,128)} %select_bitcast_fusion.6), channel_id=1, source_target_pairs={{4,0},{8,4},{12,8},{16,12},{20,16},{24,20},{28,24},{5,1},{9,5},{13... | collective-permute-start | bytes 69128 | tf_op jit(solution)/shard_map/ppermute | solution.py:42
  32.5 0.8 constant_dynamic-update-slice_fusion.2
  33.3 0.8 constant_dynamic-update-slice_fusion.1
  34.1 2.8 %gather_fusion.7 = f32[1024,60]{1,0:T(8,128)S(1)} fusion(f32[60,1344]{0,1:T(8,128)S(1)} %constant_dynamic-update-slice_fusion, s32[1024]{0:T(1024)S(1)} %get-tuple-element.118), kind=kCustom, calls=%fused_computation.2.clone | custom fusion | bytes 495616 | tf_op jit(solution)/shard_map/jit(_take)/gather | solution.py:147
  47.2 1.3 %collective-permute-start.9 = (f32[60,1,32]{0,2,1:T(8,128)S(1)}, f32[60,1,32]{0,2,1:T(8,128)S(1)}, u32[]{:S(2)}, u32[]{:S(2)}) collective-permute-start(f32[60,1,32]{0,2,1:T(8,128)S(1)} %get-tuple-element.100), channel_id=1, source_target_pairs={{0,3},{1,2},{2,1},{3,0},{4,7},{5,6},{6,5},{7,4},{8,11},{9,10},{10,... | collective-permute-start | bytes 23048 | tf_op jit(solution)/shard_map/ppermute | solution.py:34
  48.5 1.5 %collective-permute-start.8 = (f32[60,1,32]{0,2,1:T(8,128)S(1)}, f32[60,1,32]{0,2,1:T(8,128)S(1)}, u32[]{:S(2)}, u32[]{:S(2)}) collective-permute-start(f32[60,1,32]{0,2,1:T(8,128)S(1)} %get-tuple-element.101), channel_id=1, source_target_pairs={{0,2},{1,3},{2,0},{3,1},{4,6},{5,7},{6,4},{7,5},{8,10},{9,11},{10,... | collective-permute-start | bytes 23048 | tf_op jit(solution)/shard_map/ppermute | solution.py:34
  50.0 1.1 collective-permute-start.7
  51.1 5.1 %collective-permute-start.5 = (f32[60,96]{0,1:T(8,128)S(1)}, f32[60,96]{0,1:T(8,128)S(1)}, u32[]{:S(2)}, u32[]{:S(2)}) collective-permute-start(f32[60,96]{0,1:T(8,128)S(1)} %select_bitcast_fusion.5), channel_id=1, source_target_pairs={{0,4},{4,8},{8,12},{12,16},{16,20},{20,24},{24,28},{1,5},{5,9},{9,... | collective-permute-start | bytes 69128 | tf_op jit(solution)/shard_map/ppermute | solution.py:42
  56.2 1.9 %collective-permute-start.6 = (f32[60,96]{0,1:T(8,128)S(1)}, f32[60,96]{0,1:T(8,128)S(1)}, u32[]{:S(2)}, u32[]{:S(2)}) collective-permute-start(f32[60,96]{0,1:T(8,128)S(1)} %select_bitcast_fusion.4), channel_id=1, source_target_pairs={{4,0},{8,4},{12,8},{16,12},{20,16},{24,20},{28,24},{5,1},{9,5},{13... | collective-permute-start | bytes 69128 | tf_op jit(solution)/shard_map/ppermute | solution.py:42
  59.0 3.6 %collective-permute-done.6 = f32[60,96]{0,1:T(8,128)S(1)} collective-permute-done((f32[60,96]{0,1:T(8,128)S(1)}, f32[60,96]{0,1:T(8,128)S(1)}, u32[]{:S(2)}, u32[]{:S(2)}) %collective-permute-start.6) | collective-permute-done | bytes 23072 | tf_op jit(solution)/shard_map/ppermute | solution.py:42
  62.5 2.8 %gather_fusion.11 = f32[1024,60]{1,0:T(8,128)S(1)} fusion(f32[60,1344]{0,1:T(8,128)S(1)} %constant_dynamic-update-slice_fusion.7, s32[1024]{0:T(1024)S(1)} %get-tuple-element.118), kind=kCustom, calls=%fused_computation.13.clone | custom fusion | bytes 495616 | tf_op jit(solution)/shard_map/jit(_take)/gather | solution.py:147
  75.7 1.3 %collective-permute-start.14 = (f32[60,1,32]{0,2,1:T(8,128)S(1)}, f32[60,1,32]{0,2,1:T(8,128)S(1)}, u32[]{:S(2)}, u32[]{:S(2)}) collective-permute-start(f32[60,1,32]{0,2,1:T(8,128)S(1)} %get-tuple-element.96), channel_id=1, source_target_pairs={{0,3},{1,2},{2,1},{3,0},{4,7},{5,6},{6,5},{7,4},{8,11},{9,10},{10,... | collective-permute-start | bytes 23048 | tf_op jit(solution)/shard_map/ppermute | solution.py:34
  77.0 1.5 %collective-permute-start.13 = (f32[60,1,32]{0,2,1:T(8,128)S(1)}, f32[60,1,32]{0,2,1:T(8,128)S(1)}, u32[]{:S(2)}, u32[]{:S(2)}) collective-permute-start(f32[60,1,32]{0,2,1:T(8,128)S(1)} %get-tuple-element.97), channel_id=1, source_target_pairs={{0,2},{1,3},{2,0},{3,1},{4,6},{5,7},{6,4},{7,5},{8,10},{9,11},{10,... | collective-permute-start | bytes 23048 | tf_op jit(solution)/shard_map/ppermute | solution.py:34
  78.5 1.1 collective-permute-start.12
  79.6 2.4 %collective-permute-start.10 = (f32[60,96]{0,1:T(8,128)S(1)}, f32[60,96]{0,1:T(8,128)S(1)}, u32[]{:S(2)}, u32[]{:S(2)}) collective-permute-start(f32[60,96]{0,1:T(8,128)S(1)} %select_bitcast_fusion.3), channel_id=1, source_target_pairs={{0,4},{4,8},{8,12},{12,16},{16,20},{20,24},{24,28},{1,5},{5,9},{9,... | collective-permute-start | bytes 69128 | tf_op jit(solution)/shard_map/ppermute | solution.py:42
  82.0 2.1 %collective-permute-start.11 = (f32[60,96]{0,1:T(8,128)S(1)}, f32[60,96]{0,1:T(8,128)S(1)}, u32[]{:S(2)}, u32[]{:S(2)}) collective-permute-start(f32[60,96]{0,1:T(8,128)S(1)} %select_bitcast_fusion.2), channel_id=1, source_target_pairs={{4,0},{8,4},{12,8},{16,12},{20,16},{24,20},{28,24},{5,1},{9,5},{13... | collective-permute-start | bytes 69128 | tf_op jit(solution)/shard_map/ppermute | solution.py:42
  85.0 3.3 %collective-permute-done.11 = f32[60,96]{0,1:T(8,128)S(1)} collective-permute-done((f32[60,96]{0,1:T(8,128)S(1)}, f32[60,96]{0,1:T(8,128)S(1)}, u32[]{:S(2)}, u32[]{:S(2)}) %collective-permute-start.11) | collective-permute-done | bytes 23072 | tf_op jit(solution)/shard_map/ppermute | solution.py:42
  88.4 2.8 %gather_fusion.15 = f32[1024,60]{1,0:T(8,128)S(1)} fusion(f32[60,1344]{0,1:T(8,128)S(1)} %constant_dynamic-update-slice_fusion.14, s32[1024]{0:T(1024)S(1)} %get-tuple-element.118), kind=kCustom, calls=%fused_computation.14.clone | custom fusion | bytes 495616 | tf_op jit(solution)/shard_map/jit(_take)/gather | solution.py:147
  103.7 1.2 %collective-permute-start.19 = (f32[60,1,32]{0,2,1:T(8,128)S(1)}, f32[60,1,32]{0,2,1:T(8,128)S(1)}, u32[]{:S(2)}, u32[]{:S(2)}) collective-permute-start(f32[60,1,32]{0,2,1:T(8,128)S(1)} %get-tuple-element.92), channel_id=1, source_target_pairs={{0,3},{1,2},{2,1},{3,0},{4,7},{5,6},{6,5},{7,4},{8,11},{9,10},{10,... | collective-permute-start | bytes 23048 | tf_op jit(solution)/shard_map/ppermute | solution.py:34
  104.9 1.5 %collective-permute-start.18 = (f32[60,1,32]{0,2,1:T(8,128)S(1)}, f32[60,1,32]{0,2,1:T(8,128)S(1)}, u32[]{:S(2)}, u32[]{:S(2)}) collective-permute-start(f32[60,1,32]{0,2,1:T(8,128)S(1)} %get-tuple-element.93), channel_id=1, source_target_pairs={{0,2},{1,3},{2,0},{3,1},{4,6},{5,7},{6,4},{7,5},{8,10},{9,11},{10,... | collective-permute-start | bytes 23048 | tf_op jit(solution)/shard_map/ppermute | solution.py:34
  106.4 1.1 collective-permute-start.17
  107.5 2.5 %collective-permute-start.15 = (f32[60,96]{0,1:T(8,128)S(1)}, f32[60,96]{0,1:T(8,128)S(1)}, u32[]{:S(2)}, u32[]{:S(2)}) collective-permute-start(f32[60,96]{0,1:T(8,128)S(1)} %select_bitcast_fusion.1), channel_id=1, source_target_pairs={{0,4},{4,8},{8,12},{12,16},{16,20},{20,24},{24,28},{1,5},{5,9},{9,... | collective-permute-start | bytes 69128 | tf_op jit(solution)/shard_map/ppermute | solution.py:42
  110.0 1.9 %collective-permute-start.16 = (f32[60,96]{0,1:T(8,128)S(1)}, f32[60,96]{0,1:T(8,128)S(1)}, u32[]{:S(2)}, u32[]{:S(2)}) collective-permute-start(f32[60,96]{0,1:T(8,128)S(1)} %select_bitcast_fusion), channel_id=1, source_target_pairs={{4,0},{8,4},{12,8},{16,12},{20,16},{24,20},{28,24},{5,1},{9,5},{13... | collective-permute-start | bytes 69128 | tf_op jit(solution)/shard_map/ppermute | solution.py:42
  112.8 3.6 %collective-permute-done.16 = f32[60,96]{0,1:T(8,128)S(1)} collective-permute-done((f32[60,96]{0,1:T(8,128)S(1)}, f32[60,96]{0,1:T(8,128)S(1)}, u32[]{:S(2)}, u32[]{:S(2)}) %collective-permute-start.16) | collective-permute-done | bytes 23072 | tf_op jit(solution)/shard_map/ppermute | solution.py:42
  116.3 2.8 %gather_fusion.19 = f32[1024,60]{1,0:T(8,128)S(1)} fusion(f32[60,1344]{0,1:T(8,128)S(1)} %constant_dynamic-update-slice_fusion.21, s32[1024]{0:T(1024)S(1)} %get-tuple-element.118), kind=kCustom, calls=%fused_computation.15.clone | custom fusion | bytes 495616 | tf_op jit(solution)/shard_map/jit(_take)/gather | solution.py:147
  (431 shorter events, 55.1 us)
Async XLA Ops:
  0.8 15.1 %copy-start.32 = (pred[128]{0:T(512)(128)(4,1)}, pred[128]{0:T(512)(128)(4,1)S(1)}, u32[]{:S(2)}) copy-start(pred[128]{0:T(512)(128)(4,1)S(1)} %compare_and_fusion.1) | copy-start | bytes 388
  9.9 5.3 %copy-start.29 = (s32[1024]{0:T(1024)}, s32[1024]{0:T(1024)S(1)}, u32[]{:S(2)}) copy-start(s32[1024]{0:T(1024)S(1)} %pad_clamp_fusion.1) | copy-start | bytes 12292
  10.0 59.2 %copy-start.11 = (f32[1,15,35]{2,0,1:T(1,128)}, f32[1,15,35]{2,0,1:T(1,128)S(1)}, u32[]{:S(2)}) copy-start(f32[1,15,35]{2,0,1:T(1,128)S(1)} %get-tuple-element.107) | copy-start | bytes 6304
  10.0 59.4 %copy-start.9 = (f32[1,15,35]{2,0,1:T(1,128)}, f32[1,15,35]{2,0,1:T(1,128)S(1)}, u32[]{:S(2)}) copy-start(f32[1,15,35]{2,0,1:T(1,128)S(1)} %get-tuple-element.108) | copy-start | bytes 6304
  10.0 59.6 %copy-start.7 = (f32[1,15,35]{2,0,1:T(1,128)}, f32[1,15,35]{2,0,1:T(1,128)S(1)}, u32[]{:S(2)}) copy-start(f32[1,15,35]{2,0,1:T(1,128)S(1)} %get-tuple-element.109) | copy-start | bytes 6304
  15.2 4.9 %copy-start.38 = (s32[2,96]{1,0:T(2,128)S(1)}, s32[2,96]{1,0:T(2,128)}, u32[]{:S(2)}) copy-start(s32[2,96]{1,0:T(2,128)} %param.30) | copy-start | bytes 2308
  16.6 3.5 %copy-start.36 = (s32[4,256]{1,0:T(4,128)S(1)}, s32[4,256]{1,0:T(4,128)}, u32[]{:S(2)}) copy-start(s32[4,256]{1,0:T(4,128)} %param.29) | copy-start | bytes 12292
  16.6 14.6 %collective-permute-start.4 = (f32[60,1,32]{0,2,1:T(8,128)}, f32[60,1,32]{0,2,1:T(8,128)S(1)}, u32[]{:S(2)}, u32[]{:S(2)}) collective-permute-start(f32[60,1,32]{0,2,1:T(8,128)} %get-tuple-element.104), channel_id=1, source_target_pairs={{0,3},{1,2},{2,1},{3,0},{4,7},{5,6},{6,5},{7,4},{8,11},{9,10},{10,... | collective-permute-start | bytes 23048 | tf_op jit(solution)/shard_map/ppermute | solution.py:34
  17.9 13.3 %collective-permute-start.3 = (f32[60,1,32]{0,2,1:T(8,128)S(1)}, f32[60,1,32]{0,2,1:T(8,128)}, u32[]{:S(2)}, u32[]{:S(2)}) collective-permute-start(f32[60,1,32]{0,2,1:T(8,128)S(1)} %get-tuple-element.105), channel_id=1, source_target_pairs={{0,2},{1,3},{2,0},{3,1},{4,6},{5,7},{6,4},{7,5},{8,10},{9,11},{10,... | collective-permute-start | bytes 23048 | tf_op jit(solution)/shard_map/ppermute | solution.py:34
  18.9 12.3 %collective-permute-start.2 = (f32[60,1,32]{0,2,1:T(8,128)S(1)}, f32[60,1,32]{0,2,1:T(8,128)}, u32[]{:S(2)}, u32[]{:S(2)}) collective-permute-start(f32[60,1,32]{0,2,1:T(8,128)S(1)} %get-tuple-element.106), channel_id=1, source_target_pairs={{0,1},{1,0},{2,3},{3,2},{4,5},{5,4},{6,7},{7,6},{8,9},{9,8},{10,11... | collective-permute-start | bytes 23048 | tf_op jit(solution)/shard_map/ppermute | solution.py:34
  20.1 25.7 %copy-start.25 = (pred[96]{0:T(512)(128)(4,1)}, pred[96]{0:T(512)(128)(4,1)S(1)}, u32[]{:S(2)}) copy-start(pred[96]{0:T(512)(128)(4,1)S(1)} %get-tuple-element.59) | copy-start | bytes 292
  20.1 23.9 %copy-start.28 = (s32[1024]{0:T(1024)}, s32[1024]{0:T(1024)S(1)}, u32[]{:S(2)}) copy-start(s32[1024]{0:T(1024)S(1)} %get-tuple-element.117) | copy-start | bytes 12292
  20.9 11.6 %collective-permute-start = (f32[60,96]{0,1:T(8,128)S(1)}, f32[60,96]{0,1:T(8,128)}, u32[]{:S(2)}, u32[]{:S(2)}) collective-permute-start(f32[60,96]{0,1:T(8,128)S(1)} %select_bitcast_fusion.7), channel_id=1, source_target_pairs={{0,4},{4,8},{8,12},{12,16},{16,20},{20,24},{24,28},{1,5},{5,9},{9,... | collective-permute-start | bytes 69128 | tf_op jit(solution)/shard_map/ppermute | solution.py:42
  25.1 18.3 %copy-start.31 = (s32[1024]{0:T(1024)}, s32[1024]{0:T(1024)S(1)}, u32[]{:S(2)}) copy-start(s32[1024]{0:T(1024)S(1)} %pad_clamp_fusion.2) | copy-start | bytes 12292
  26.4 6.9 %collective-permute-start.1 = (f32[60,96]{0,1:T(8,128)}, f32[60,96]{0,1:T(8,128)}, u32[]{:S(2)}, u32[]{:S(2)}) collective-permute-start(f32[60,96]{0,1:T(8,128)} %select_bitcast_fusion.6), channel_id=1, source_target_pairs={{4,0},{8,4},{12,8},{16,12},{20,16},{24,20},{28,24},{5,1},{9,5},{13... | collective-permute-start | bytes 69128 | tf_op jit(solution)/shard_map/ppermute | solution.py:42
  28.6 8.4 %copy-start.16 = (pred[1024]{0:T(1024)(128)(4,1)}, pred[1024]{0:T(1024)(128)(4,1)S(1)}, u32[]{:S(2)}) copy-start(pred[1024]{0:T(1024)(128)(4,1)S(1)} %compare_and_fusion) | copy-start | bytes 3076
  47.2 11.0 %collective-permute-start.9 = (f32[60,1,32]{0,2,1:T(8,128)S(1)}, f32[60,1,32]{0,2,1:T(8,128)S(1)}, u32[]{:S(2)}, u32[]{:S(2)}) collective-permute-start(f32[60,1,32]{0,2,1:T(8,128)S(1)} %get-tuple-element.100), channel_id=1, source_target_pairs={{0,3},{1,2},{2,1},{3,0},{4,7},{5,6},{6,5},{7,4},{8,11},{9,10},{10,... | collective-permute-start | bytes 23048 | tf_op jit(solution)/shard_map/ppermute | solution.py:34
  48.5 9.7 %collective-permute-start.8 = (f32[60,1,32]{0,2,1:T(8,128)S(1)}, f32[60,1,32]{0,2,1:T(8,128)S(1)}, u32[]{:S(2)}, u32[]{:S(2)}) collective-permute-start(f32[60,1,32]{0,2,1:T(8,128)S(1)} %get-tuple-element.101), channel_id=1, source_target_pairs={{0,2},{1,3},{2,0},{3,1},{4,6},{5,7},{6,4},{7,5},{8,10},{9,11},{10,... | collective-permute-start | bytes 23048 | tf_op jit(solution)/shard_map/ppermute | solution.py:34
  50.0 8.2 %collective-permute-start.7 = (f32[60,1,32]{0,2,1:T(8,128)S(1)}, f32[60,1,32]{0,2,1:T(8,128)S(1)}, u32[]{:S(2)}, u32[]{:S(2)}) collective-permute-start(f32[60,1,32]{0,2,1:T(8,128)S(1)} %get-tuple-element.102), channel_id=1, source_target_pairs={{0,1},{1,0},{2,3},{3,2},{4,5},{5,4},{6,7},{7,6},{8,9},{9,8},{10,11... | collective-permute-start | bytes 23048 | tf_op jit(solution)/shard_map/ppermute | solution.py:34
  51.1 7.8 %collective-permute-start.5 = (f32[60,96]{0,1:T(8,128)S(1)}, f32[60,96]{0,1:T(8,128)S(1)}, u32[]{:S(2)}, u32[]{:S(2)}) collective-permute-start(f32[60,96]{0,1:T(8,128)S(1)} %select_bitcast_fusion.5), channel_id=1, source_target_pairs={{0,4},{4,8},{8,12},{12,16},{16,20},{20,24},{24,28},{1,5},{5,9},{9,... | collective-permute-start | bytes 69128 | tf_op jit(solution)/shard_map/ppermute | solution.py:42
  56.2 6.3 %collective-permute-start.6 = (f32[60,96]{0,1:T(8,128)S(1)}, f32[60,96]{0,1:T(8,128)S(1)}, u32[]{:S(2)}, u32[]{:S(2)}) collective-permute-start(f32[60,96]{0,1:T(8,128)S(1)} %select_bitcast_fusion.4), channel_id=1, source_target_pairs={{4,0},{8,4},{12,8},{16,12},{20,16},{24,20},{28,24},{5,1},{9,5},{13... | collective-permute-start | bytes 69128 | tf_op jit(solution)/shard_map/ppermute | solution.py:42
  75.7 8.6 %collective-permute-start.14 = (f32[60,1,32]{0,2,1:T(8,128)S(1)}, f32[60,1,32]{0,2,1:T(8,128)S(1)}, u32[]{:S(2)}, u32[]{:S(2)}) collective-permute-start(f32[60,1,32]{0,2,1:T(8,128)S(1)} %get-tuple-element.96), channel_id=1, source_target_pairs={{0,3},{1,2},{2,1},{3,0},{4,7},{5,6},{6,5},{7,4},{8,11},{9,10},{10,... | collective-permute-start | bytes 23048 | tf_op jit(solution)/shard_map/ppermute | solution.py:34
  77.0 7.3 %collective-permute-start.13 = (f32[60,1,32]{0,2,1:T(8,128)S(1)}, f32[60,1,32]{0,2,1:T(8,128)S(1)}, u32[]{:S(2)}, u32[]{:S(2)}) collective-permute-start(f32[60,1,32]{0,2,1:T(8,128)S(1)} %get-tuple-element.97), channel_id=1, source_target_pairs={{0,2},{1,3},{2,0},{3,1},{4,6},{5,7},{6,4},{7,5},{8,10},{9,11},{10,... | collective-permute-start | bytes 23048 | tf_op jit(solution)/shard_map/ppermute | solution.py:34
  78.5 5.8 %collective-permute-start.12 = (f32[60,1,32]{0,2,1:T(8,128)S(1)}, f32[60,1,32]{0,2,1:T(8,128)S(1)}, u32[]{:S(2)}, u32[]{:S(2)}) collective-permute-start(f32[60,1,32]{0,2,1:T(8,128)S(1)} %get-tuple-element.98), channel_id=1, source_target_pairs={{0,1},{1,0},{2,3},{3,2},{4,5},{5,4},{6,7},{7,6},{8,9},{9,8},{10,11... | collective-permute-start | bytes 23048 | tf_op jit(solution)/shard_map/ppermute | solution.py:34
  79.6 5.4 %collective-permute-start.10 = (f32[60,96]{0,1:T(8,128)S(1)}, f32[60,96]{0,1:T(8,128)S(1)}, u32[]{:S(2)}, u32[]{:S(2)}) collective-permute-start(f32[60,96]{0,1:T(8,128)S(1)} %select_bitcast_fusion.3), channel_id=1, source_target_pairs={{0,4},{4,8},{8,12},{12,16},{16,20},{20,24},{24,28},{1,5},{5,9},{9,... | collective-permute-start | bytes 69128 | tf_op jit(solution)/shard_map/ppermute | solution.py:42
  82.0 6.3 %collective-permute-start.11 = (f32[60,96]{0,1:T(8,128)S(1)}, f32[60,96]{0,1:T(8,128)S(1)}, u32[]{:S(2)}, u32[]{:S(2)}) collective-permute-start(f32[60,96]{0,1:T(8,128)S(1)} %select_bitcast_fusion.2), channel_id=1, source_target_pairs={{4,0},{8,4},{12,8},{16,12},{20,16},{24,20},{28,24},{5,1},{9,5},{13... | collective-permute-start | bytes 69128 | tf_op jit(solution)/shard_map/ppermute | solution.py:42
  103.7 8.3 %collective-permute-start.19 = (f32[60,1,32]{0,2,1:T(8,128)S(1)}, f32[60,1,32]{0,2,1:T(8,128)S(1)}, u32[]{:S(2)}, u32[]{:S(2)}) collective-permute-start(f32[60,1,32]{0,2,1:T(8,128)S(1)} %get-tuple-element.92), channel_id=1, source_target_pairs={{0,3},{1,2},{2,1},{3,0},{4,7},{5,6},{6,5},{7,4},{8,11},{9,10},{10,... | collective-permute-start | bytes 23048 | tf_op jit(solution)/shard_map/ppermute | solution.py:34
  104.9 7.1 %collective-permute-start.18 = (f32[60,1,32]{0,2,1:T(8,128)S(1)}, f32[60,1,32]{0,2,1:T(8,128)S(1)}, u32[]{:S(2)}, u32[]{:S(2)}) collective-permute-start(f32[60,1,32]{0,2,1:T(8,128)S(1)} %get-tuple-element.93), channel_id=1, source_target_pairs={{0,2},{1,3},{2,0},{3,1},{4,6},{5,7},{6,4},{7,5},{8,10},{9,11},{10,... | collective-permute-start | bytes 23048 | tf_op jit(solution)/shard_map/ppermute | solution.py:34
  106.4 5.6 %collective-permute-start.17 = (f32[60,1,32]{0,2,1:T(8,128)S(1)}, f32[60,1,32]{0,2,1:T(8,128)S(1)}, u32[]{:S(2)}, u32[]{:S(2)}) collective-permute-start(f32[60,1,32]{0,2,1:T(8,128)S(1)} %get-tuple-element.94), channel_id=1, source_target_pairs={{0,1},{1,0},{2,3},{3,2},{4,5},{5,4},{6,7},{7,6},{8,9},{9,8},{10,11... | collective-permute-start | bytes 23048 | tf_op jit(solution)/shard_map/ppermute | solution.py:34
  107.5 5.2 %collective-permute-start.15 = (f32[60,96]{0,1:T(8,128)S(1)}, f32[60,96]{0,1:T(8,128)S(1)}, u32[]{:S(2)}, u32[]{:S(2)}) collective-permute-start(f32[60,96]{0,1:T(8,128)S(1)} %select_bitcast_fusion.1), channel_id=1, source_target_pairs={{0,4},{4,8},{8,12},{12,16},{16,20},{20,24},{24,28},{1,5},{5,9},{9,... | collective-permute-start | bytes 69128 | tf_op jit(solution)/shard_map/ppermute | solution.py:42
  110.0 6.3 %collective-permute-start.16 = (f32[60,96]{0,1:T(8,128)S(1)}, f32[60,96]{0,1:T(8,128)S(1)}, u32[]{:S(2)}, u32[]{:S(2)}) collective-permute-start(f32[60,96]{0,1:T(8,128)S(1)} %select_bitcast_fusion), channel_id=1, source_target_pairs={{4,0},{8,4},{12,8},{16,12},{20,16},{24,20},{28,24},{5,1},{9,5},{13... | collective-permute-start | bytes 69128 | tf_op jit(solution)/shard_map/ppermute | solution.py:42
  116.3 2.8 %copy-start.18 = (pred[1024]{0:T(1024)(128)(4,1)S(1)}, pred[1024]{0:T(1024)(128)(4,1)}, u32[]{:S(2)}) copy-start(pred[1024]{0:T(1024)(128)(4,1)} %copy-done.16) | copy-start | bytes 3076
  (30 other events, 24.4 us)
